TPU v7x, 32 devices: a whole 2x2x4 slice. The times are simulated.
32 devices in a mesh: dp: 8 (over y, x, core), tensor: 4 (over z).
Axes of the slice: x: 2, y: 2, z: 4, core: 2. Of those that a mesh axis runs over, the one named last changes fastest.
Arguments:
- hidden_in: bfloat16 [3072, 4096], P('dp', 'tensor'), may hold values from -48 to 48
- encodings: bfloat16 [512, 128, 896], P('dp', 'tensor'), may hold values from -48 to 48
- nbr_shard: int32 [48, 2], P('dp'), may hold values from 0 to 7, all different within a row; in each aligned block of 6 rows (0 to 5, 6 to 11, ...) at most 3 rows name the same one
- nbr_row: int32 [48, 2], P('dp'), may hold values from 0 to 63
- w_query: bfloat16 [4096, 4096], P(None, 'tensor'), may hold values from -0.09375 to 0.09375
- w_key: bfloat16 [896, 4096], P(None, 'tensor'), may hold values from -0.1875 to 0.1875
- w_value: bfloat16 [896, 4096], P(None, 'tensor'), may hold values from -0.1875 to 0.1875
- w_output: bfloat16 [4096, 4096], P('tensor'), may hold values from -0.09375 to 0.09375
- cotangent: bfloat16 [3072, 4096], P('dp', 'tensor'), may hold values from -6 to 6
Outputs:
- layer_out: bfloat16 [3072, 4096], P('dp', 'tensor')
- grad_hidden: bfloat16 [3072, 4096], P('dp', 'tensor')
- grad_encodings: float32 [512, 128, 896], P('dp', 'tensor')
- grad_query: float32 [4096, 4096], P('dp', 'tensor')
- grad_key: float32 [896, 4096], P('dp', 'tensor')
- grad_value: float32 [896, 4096], P('dp', 'tensor')
- grad_output: float32 [4096, 4096], P('tensor', 'dp')
Inputs may be any that keep to these rules, and one draw needn't show every extreme that they name: `nbr_shard`: in the 6 spans of one index of dp no shard is named more than 3 times, and one is named exactly 3 times in some of them; the 2 shards of a span differ.
All inputs are finite; a program needn't handle non-finite values.
Results may differ from a plain program's by a relative error of at most 0.02.
Values may be sent and summed in bfloat16 or wider, within the bound.
No kernel may reach another device: no remote copies, remote signals or barrier semaphores. Data moves between devices by JAX's collectives and lax.ppermute only.
A program may use at most 128 MiB of HBM per device.

v0:
```python
import math

import jax
import jax.numpy as jnp
from jax import lax
from jax.sharding import PartitionSpec as P

HD = 128
SPAN = 64
NB = 128
K_NBR = 2


def shards(hidden_in, encodings, nbr_shard, nbr_row, w_query, w_key, w_value, w_output, cotangent):
    n_shards = lax.axis_size("dp")
    tok_rows = hidden_in.shape[0]
    columns = w_query.shape[1]
    heads_here = columns // HD
    span_count = tok_rows // SPAN
    live_blocks = K_NBR * span_count
    capacity = max(2, 4 * span_count // n_shards)
    slot_count = n_shards * capacity
    db_blocks = encodings.shape[0]
    block_part = encodings.shape[1]
    width = encodings.shape[2]
    scale = 1.0 / math.sqrt(HD)
    owners = nbr_shard.reshape(live_blocks)
    rowids = nbr_row.reshape(live_blocks)
    order = jnp.arange(live_blocks, dtype=jnp.int32)
    earlier = (owners[:, None] == owners[None, :]) & (order[None, :] < order[:, None])
    position = jnp.sum(earlier.astype(jnp.int32), axis=1)
    slot_of = owners * capacity + position
    picked = slot_of[:, None] == jnp.arange(slot_count, dtype=jnp.int32)[None, :]
    request = jnp.sum(jnp.where(picked, rowids[:, None] + 1, 0), axis=0) - 1
    wanted = lax.all_to_all(
        request.reshape(n_shards, capacity), "dp", split_axis=0, concat_axis=0, tiled=True
    )
    table = (
        wanted.reshape(slot_count)[:, None] == jnp.arange(db_blocks, dtype=jnp.int32)[None, :]
    ).astype(jnp.bfloat16)
    outgoing = jnp.dot(
        table, encodings.reshape(db_blocks, block_part * width), preferred_element_type=jnp.float32
    )
    outgoing = outgoing.astype(jnp.bfloat16).reshape(n_shards, capacity, block_part, width)
    arrived = lax.all_to_all(outgoing, "dp", split_axis=0, concat_axis=0, tiled=True).reshape(
        slot_count, block_part, width
    )
    select = picked.astype(jnp.bfloat16)
    gathered = lax.all_gather(arrived, "tensor", axis=1, tiled=True)
    neighbours = jnp.dot(
        select, gathered.reshape(slot_count, NB * width), preferred_element_type=jnp.float32
    )
    neighbours = neighbours.astype(jnp.bfloat16)
    nbr_flat = neighbours.reshape(live_blocks * NB, width)
    hidden_full = lax.all_gather(hidden_in, "tensor", axis=1, tiled=True)
    query = jnp.dot(hidden_full, w_query, preferred_element_type=jnp.float32).astype(jnp.bfloat16)
    keys = jnp.dot(nbr_flat, w_key, preferred_element_type=jnp.float32).astype(jnp.bfloat16)
    values = jnp.dot(nbr_flat, w_value, preferred_element_type=jnp.float32).astype(jnp.bfloat16)
    query_h = query.reshape(span_count, SPAN, heads_here, HD)
    keys_h = keys.reshape(span_count, K_NBR * NB, heads_here, HD)
    values_h = values.reshape(span_count, K_NBR * NB, heads_here, HD)
    scores = (
        jnp.einsum("cqhd,ckhd->chqk", query_h, keys_h, preferred_element_type=jnp.float32) * scale
    )
    probs = jax.nn.softmax(scores, axis=-1)
    probs_b = probs.astype(jnp.bfloat16)
    attended = jnp.einsum("chqk,ckhd->cqhd", probs_b, values_h, preferred_element_type=jnp.float32)
    attended = attended.astype(jnp.bfloat16).reshape(tok_rows, columns)
    out_terms = jnp.dot(attended, w_output, preferred_element_type=jnp.float32)
    layer_out = lax.psum_scatter(out_terms, "tensor", scatter_dimension=1, tiled=True).astype(
        jnp.bfloat16
    )
    grad_full = lax.all_gather(cotangent, "tensor", axis=1, tiled=True)
    grad_att = jnp.dot(grad_full, w_output.T, preferred_element_type=jnp.float32).astype(
        jnp.bfloat16
    )
    grad_output = jnp.dot(attended.T, grad_full, preferred_element_type=jnp.float32)
    grad_att_h = grad_att.reshape(span_count, SPAN, heads_here, HD)
    grad_prob = jnp.einsum(
        "cqhd,ckhd->chqk", grad_att_h, values_h, preferred_element_type=jnp.float32
    )
    inner = jnp.sum(grad_prob * probs, axis=-1, keepdims=True)
    grad_score = (probs * (grad_prob - inner) * scale).astype(jnp.bfloat16)
    grad_v = jnp.einsum("chqk,cqhd->ckhd", probs_b, grad_att_h, preferred_element_type=jnp.float32)
    grad_v = grad_v.astype(jnp.bfloat16).reshape(live_blocks * NB, columns)
    grad_q = jnp.einsum("chqk,ckhd->cqhd", grad_score, keys_h, preferred_element_type=jnp.float32)
    grad_q = grad_q.astype(jnp.bfloat16).reshape(tok_rows, columns)
    grad_k = jnp.einsum("chqk,cqhd->ckhd", grad_score, query_h, preferred_element_type=jnp.float32)
    grad_k = grad_k.astype(jnp.bfloat16).reshape(live_blocks * NB, columns)
    hidden_terms = jnp.dot(grad_q, w_query.T, preferred_element_type=jnp.float32)
    grad_hidden = lax.psum_scatter(hidden_terms, "tensor", scatter_dimension=1, tiled=True).astype(
        jnp.bfloat16
    )
    grad_query = jnp.dot(hidden_full.T, grad_q, preferred_element_type=jnp.float32)
    grad_key = jnp.dot(nbr_flat.T, grad_k, preferred_element_type=jnp.float32)
    grad_value = jnp.dot(nbr_flat.T, grad_v, preferred_element_type=jnp.float32)
    nbr_terms = jnp.dot(grad_k, w_key.T, preferred_element_type=jnp.float32)
    nbr_terms = nbr_terms + jnp.dot(grad_v, w_value.T, preferred_element_type=jnp.float32)
    spread_table = picked.astype(jnp.float32).T
    spread = jnp.dot(
        spread_table, nbr_terms.reshape(live_blocks, NB * width), precision=lax.Precision.HIGHEST
    )
    share = lax.psum_scatter(
        spread.reshape(slot_count, NB, width).astype(jnp.bfloat16),
        "tensor",
        scatter_dimension=1,
        tiled=True,
    ).astype(jnp.float32)
    slot_grad = share.reshape(slot_count, block_part * width)
    returned = lax.all_to_all(
        slot_grad.reshape(n_shards, capacity, block_part, width),
        "dp",
        split_axis=0,
        concat_axis=0,
        tiled=True,
    )
    grad_encodings = jnp.dot(
        table.astype(jnp.float32).T,
        returned.reshape(slot_count, block_part * width),
        precision=lax.Precision.HIGHEST,
    )
    grad_encodings = grad_encodings.reshape(db_blocks, block_part, width)
    summed_q, summed_k, summed_v, summed_o = (
        lax.psum_scatter(
            grad_query.astype(jnp.bfloat16), "dp", scatter_dimension=0, tiled=True
        ).astype(jnp.float32),
        lax.psum_scatter(
            grad_key.astype(jnp.bfloat16), "dp", scatter_dimension=0, tiled=True
        ).astype(jnp.float32),
        lax.psum_scatter(
            grad_value.astype(jnp.bfloat16), "dp", scatter_dimension=0, tiled=True
        ).astype(jnp.float32),
        lax.psum_scatter(
            grad_output.astype(jnp.bfloat16), "dp", scatter_dimension=1, tiled=True
        ).astype(jnp.float32),
    )
    return (layer_out, grad_hidden, grad_encodings, summed_q, summed_k, summed_v, summed_o)


def solution(mesh):
    return jax.shard_map(
        shards,
        mesh=mesh,
        in_specs=(
            P("dp", "tensor"),
            P("dp", "tensor", None),
            P("dp", None),
            P("dp", None),
            P(None, "tensor"),
            P(None, "tensor"),
            P(None, "tensor"),
            P("tensor", None),
            P("dp", "tensor"),
        ),
        out_specs=(
            P("dp", "tensor"),
            P("dp", "tensor"),
            P("dp", "tensor", None),
            P("dp", "tensor"),
            P("dp", "tensor"),
            P("dp", "tensor"),
            P("tensor", "dp"),
        ),
        check_vma=False,
    )
```

profile of v0, /device:TPU:0, one launch (start us, length us, event | category | flops | bytes accessed | tf_op | source)
XLA Modules:
  0.0 944.5 jit_solution(16228222563790149321)
XLA Ops:
  16.6 5.2 copy.89
  26.0 22.9 %all_to_all.16 = bf16[8,3,32,896]{3,2,1,0:T(8,128)(2,1)} all-to-all(bf16[8,3,32,896]{3,2,1,0:T(8,128)(2,1)S(1)} %bitcast.123), channel_id=1, replica_groups=mesh['dp'=8,'tensor'=4] {'dp'}, dimensions={0} | all-to-all | bytes 2752512 | tf_op jit(solution)/shard_map/all_to_all | solution.py:45
  49.5 26.3 %all-gather.8.cloned.1.call-done = bf16[384,4096]{1,0:T(8,128)(2,1)} async-done(((bf16[384,1024]{1,0:T(8,128)(2,1)}), bf16[384,4096]{1,0:T(8,128)(2,1)}) %all-gather.8.cloned.1.call-update) | async-done | bytes 3145744 | tf_op jit(solution)/shard_map/all_gather | solution.py:73
  75.8 7.8 fusion.62
  83.7 55.7 %all-gather.6.cloned.1.call-done = bf16[384,4096]{1,0:T(8,128)(2,1)} async-done(((bf16[384,1024]{1,0:T(8,128)(2,1)}), bf16[384,4096]{1,0:T(8,128)(2,1)}) %all-gather.6.cloned.1.call-update) | async-done | bytes 3145744 | tf_op jit(solution)/shard_map/all_gather | solution.py:55
  139.4 7.7 fusion.61
  147.4 94.7 %all-gather.4.cloned.1.call-done = bf16[24,128,896]{2,1,0:T(8,128)(2,1)} async-done(((bf16[24,32,896]{2,1,0:T(8,128)(2,1)}), bf16[24,128,896]{2,1,0:T(8,128)(2,1)}) %all-gather.4.cloned.1.call-update) | async-done | bytes 5505040 | tf_op jit(solution)/shard_map/all_gather | solution.py:49
  242.1 5.7 copy.91
  255.9 5.4 fusion.36
  275.2 10.4 %convert_bitcast_fusion.1 = bf16[6,256,8,128]{1,3,2,0:T(8,128)(2,1)} fusion(bf16[6,64,8,128]{3,2,1,0:T(8,128)(2,1)S(1)} %bitcast.126, f32[6,8,64]{2,1,0:T(8,128)S(1)} %get-tuple-element.35, f32[6,8,64,256]{3,2,1,0:T(8,128)} %copy-done.4), kind=kOutput, calls=%fused_computation.20 | convolution fusion | flops 206834944 | bytes 7090176 | tf_op jit(solution)/shard_map/chqk,cqhd->ckhd/dot_general | solution.py:84
  285.6 23.0 %convert_bitcast_fusion.2 = bf16[6,256,8,128]{1,3,2,0:T(8,128)(2,1)} fusion(f32[6,8,64,256]{3,2,1,0:T(8,128)} %fusion.19, bf16[6,64,8,128]{3,2,1,0:T(8,128)(2,1)S(1)} %bitcast.128, f32[6,8,64,256]{3,2,1,0:T(8,128)} %get-tuple-element.36, f32[6,8,64]{2,1,0:T(8,128)S(1)} %get-tuple-element.35), kind=kOutput, calls=%fused_computation.21 | convolution fusion | flops 208407808 | bytes 10235904 | tf_op jit(solution)/shard_map/chqk,cqhd->ckhd/dot_general | solution.py:88
  318.8 5.5 fusion.12
  324.3 5.3 convolution_add_fusion
  329.7 5.7 reshape.120
  340.3 9.4 fusion.4
  350.0 7.0 fusion.44
  357.0 7.0 fusion.41
  364.1 9.3 fusion.58
  374.0 8.8 convolution_convert_fusion.2
  383.1 22.5 %fusion.63 = bf16[6,64,8,128]{3,1,2,0:T(8,128)(2,1)S(1)} fusion(bf16[6,256,8,128]{3,2,1,0:T(8,128)(2,1)} %bitcast.116, f32[6,8,64,256]{3,2,1,0:T(8,128)} %fusion.19, f32[6,8,64,256]{3,2,1,0:T(8,128)} %get-tuple-element.36, f32[6,8,64]{2,1,0:T(8,128)S(1)} %get-tuple-element.35), kind=kOutput, calls=%fused_computation.58 | convolution fusion | flops 207228160 | bytes 10235904 | tf_op jit(solution)/shard_map/chqk,ckhd->cqhd/dot_general | solution.py:86
  406.2 8.8 convert_bitcast_fusion
  415.0 10.9 %fusion.69 = f32[384,4096]{1,0:T(8,128)} fusion(bf16[4096,1024]{1,0:T(8,128)(2,1)} %param.13, bf16[48,8,8,128]{3,2,1,0:T(8,128)(2,1)S(1)} %bitcast.136), kind=kOutput, calls=%fused_computation.60 | convolution fusion | flops 3221225472 | bytes 15466496 | tf_op jit(solution)/shard_map/dot_general | solution.py:90
  426.0 8.7 fusion.72
  434.8 11.5 %reduce-scatter.12.cloned.1.call-done = bf16[24,32,896]{2,0,1:T(8,128)(2,1)} async-done(((bf16[24,128,896]{2,0,1:T(8,128)(2,1)}), bf16[24,32,896]{2,0,1:T(8,128)(2,1)}) %reduce-scatter.12.cloned.1.call-update) | async-done | bytes 1376272 | tf_op jit(solution)/shard_map/reduce_scatter | solution.py:103
  454.1 46.8 %reduce-scatter.18.cloned.1.call-done = bf16[112,1024]{1,0:T(8,128)(2,1)} async-done(((bf16[896,1024]{1,0:T(8,128)(2,1)}), bf16[112,1024]{1,0:T(8,128)(2,1)}) %reduce-scatter.18.cloned.1.call-update) | async-done | bytes 229392 | tf_op jit(solution)/shard_map/reduce_scatter | solution.py:130
  502.6 41.6 %reduce-scatter.16.cloned.1.call-done = bf16[112,1024]{1,0:T(8,128)(2,1)} async-done(((bf16[896,1024]{1,0:T(8,128)(2,1)}), bf16[112,1024]{1,0:T(8,128)(2,1)}) %reduce-scatter.16.cloned.1.call-update) | async-done | bytes 229392 | tf_op jit(solution)/shard_map/reduce_scatter | solution.py:127
  546.0 73.0 %reduce-scatter.20.cloned.1.call-done = bf16[1024,512]{1,0:T(8,128)(2,1)} async-done(((bf16[1024,4096]{1,0:T(8,128)(2,1)}), bf16[1024,512]{1,0:T(8,128)(2,1)}) %reduce-scatter.20.cloned.1.call-update) | async-done | bytes 1048592 | tf_op jit(solution)/shard_map/reduce_scatter | solution.py:133
  621.9 72.0 %reduce-scatter.14.cloned.1.call-done = bf16[512,1024]{0,1:T(8,128)(2,1)} async-done(((bf16[4096,1024]{0,1:T(8,128)(2,1)}), bf16[512,1024]{0,1:T(8,128)(2,1)}) %reduce-scatter.14.cloned.1.call-update) | async-done | bytes 1048592 | tf_op jit(solution)/shard_map/reduce_scatter | solution.py:124
  696.4 110.6 %reduce-scatter.10.cloned.1.call-done = f32[384,1024]{1,0:T(8,128)} async-done(((f32[384,4096]{1,0:T(8,128)}), f32[384,1024]{1,0:T(8,128)}) %reduce-scatter.10.cloned.1.call-update) | async-done | bytes 1572880 | tf_op jit(solution)/shard_map/reduce_scatter | solution.py:91
  809.4 111.6 %reduce-scatter.8.cloned.1.call-done = f32[384,1024]{1,0:T(8,128)} async-done(((f32[384,4096]{1,0:T(8,128)}), f32[384,1024]{1,0:T(8,128)}) %reduce-scatter.8.cloned.1.call-update) | async-done | bytes 1572880 | tf_op jit(solution)/shard_map/reduce_scatter | solution.py:70
  923.4 6.5 fusion.28
  930.0 7.3 copy.85
  (84 shorter events, 74.7 us)
Async XLA Ops:
  7.2 248.8 %copy-start = (bf16[896,1024]{1,0:T(8,128)(2,1)S(1)}, bf16[896,1024]{1,0:T(8,128)(2,1)}, u32[]{:S(2)}) copy-start(bf16[896,1024]{1,0:T(8,128)(2,1)} %param.14) | copy-start | bytes 5505028
  7.2 68.6 %all-gather.8.cloned.1.call-start = ((), (), s32[]{:S(2)}) async-start(), calls=%async_computation.13 | async-start | bytes 3932160 | tf_op jit(solution)/shard_map/all_gather | solution.py:73
  7.9 131.5 %all-gather.6.cloned.1.call-start = ((), (), s32[]{:S(2)}) async-start(), calls=%async_computation.11 | async-start | bytes 3932160 | tf_op jit(solution)/shard_map/all_gather | solution.py:55
  11.3 10.5 %all-to-all-start = ((s32[8,1,3]{2,1,0:T(1,128)}), s32[8,1,3]{2,1,0:T(1,128)S(1)}, u32[]{:S(2)}, u32[]{:S(2)}) async-start(s32[8,1,3]{2,1,0:T(1,128)} %bitcast), calls=%async_computation | async-start | bytes 8192 | tf_op jit(solution)/shard_map/all_to_all | solution.py:35
  16.5 225.5 %all-gather.4.cloned.1.call-start = ((), (), s32[]{:S(2)}) async-start(), calls=%async_computation.10 | async-start | bytes 6881280 | tf_op jit(solution)/shard_map/all_gather | solution.py:49
  23.1 2.9 copy-start.7
  48.9 397.3 %reduce-scatter.12.cloned.1.call-start = ((), (), s32[]{:S(2)}) async-start(), calls=%async_computation.15 | async-start | bytes 6881280 | tf_op jit(solution)/shard_map/reduce_scatter | solution.py:103
  261.4 1.8 copy-start.6
  261.4 2.3 copy-start.9
  263.7 4.7 copy-start.2
  268.3 3.9 copy-start.3
  269.6 2.7 copy-start.4
  318.7 5.6 copy-start.5
  318.8 5.6 copy-start.10
  349.7 151.2 %reduce-scatter.18.cloned.1.call-start = ((), (), s32[]{:S(2)}) async-start(), calls=%async_computation.18 | async-start | bytes 2064384 | tf_op jit(solution)/shard_map/reduce_scatter | solution.py:130
  357.0 187.3 %reduce-scatter.16.cloned.1.call-start = ((), (), s32[]{:S(2)}) async-start(), calls=%async_computation.17 | async-start | bytes 2064384 | tf_op jit(solution)/shard_map/reduce_scatter | solution.py:127
  364.1 255.0 %reduce-scatter.20.cloned.1.call-start = ((), (), s32[]{:S(2)}) async-start(), calls=%async_computation.19 | async-start | bytes 9437184 | tf_op jit(solution)/shard_map/reduce_scatter | solution.py:133
  382.8 311.0 %reduce-scatter.14.cloned.1.call-start = ((), (), s32[]{:S(2)}) async-start(), calls=%async_computation.16 | async-start | bytes 9437184 | tf_op jit(solution)/shard_map/reduce_scatter | solution.py:124
  415.0 392.0 %reduce-scatter.10.cloned.1.call-start = ((), (), s32[]{:S(2)}) async-start(), calls=%async_computation.14 | async-start | bytes 7864320 | tf_op jit(solution)/shard_map/reduce_scatter | solution.py:91
  426.0 495.0 %reduce-scatter.8.cloned.1.call-start = ((), (), s32[]{:S(2)}) async-start(), calls=%async_computation.12 | async-start | bytes 7864320 | tf_op jit(solution)/shard_map/reduce_scatter | solution.py:70
  449.4 474.0 %all-to-all-start.2 = ((f32[8,3,32,896]{3,2,1,0:T(8,128)}), f32[8,3,32,896]{3,2,1,0:T(8,128)}, u32[]{:S(2)}, u32[]{:S(2)}) async-start(f32[8,3,32,896]{3,2,1,0:T(8,128)} %bitcast.119), calls=%async_computation.5 | async-start | bytes 5505024 | tf_op jit(solution)/shard_map/all_to_all | solution.py:110
  696.4 227.0 %copy-start.8 = (s32[24]{0:T(128)S(1)}, s32[24]{0:T(128)}, u32[]{:S(2)}) copy-start(s32[24]{0:T(128)} %copy-done.7) | copy-start | bytes 292
  929.9 7.3 copy-start.1
Sparse Core Ops, SparseCore 0:
  9.6 66.1 all-gather.7
  77.3 62.0 all-gather.5
  141.0 100.9 all-gather.3
  349.9 96.3 reduce-scatter.11
  450.0 50.8 reduce-scatter.17
  504.7 39.5 reduce-scatter.15
  547.7 71.2 reduce-scatter.19
  622.5 71.2 reduce-scatter.13
  696.2 110.7 reduce-scatter.9
  809.7 111.2 reduce-scatter.7
where the time goes:
time: 948 us; the launch traced here: 945 us
  waiting for transfers between devices  645 us (68%)
  matrix products  178 us (19%)
  local copies, waits for them, and re-layouts  56.6 us (6%)
  blocking collectives  22.9 us (2%)
  other arithmetic  15.5 us (2%)
  between operations  14.9 us (2%)
  starting transfers between devices  11.2 us (1%)
    reduce_scatter x1, waiting for transfers between devices, shards(): lax.psum_scatter(out_terms, 'tensor', scatter_dimension=1, tiled=True)  112 us
    reduce_scatter x1, waiting for transfers between devices, shards(): lax.psum_scatter(hidden_terms, 'tensor', scatter_dimension=1, tiled=True)  111 us
    all_gather x1, waiting for transfers between devices, shards(): gathered = lax.all_gather(arrived, 'tensor', axis=1, tiled=True)  94.7 us
    reduce_scatter x1, waiting for transfers between devices, shards(): lax.psum_scatter(grad_output.astype(jnp.bfloat16), 'dp', scatter_dimensio...  73 us
    reduce_scatter x1, waiting for transfers between devices, shards(): lax.psum_scatter(grad_query.astype(jnp.bfloat16), 'dp', scatter_dimension...  72 us
    all_gather x1, waiting for transfers between devices, shards(): hidden_full = lax.all_gather(hidden_in, 'tensor', axis=1, tiled=True)  55.7 us
    reduce_scatter x1, waiting for transfers between devices, shards(): lax.psum_scatter(grad_value.astype(jnp.bfloat16), 'dp', scatter_dimension...  46.8 us
    reduce_scatter x1, waiting for transfers between devices, shards(): lax.psum_scatter(grad_key.astype(jnp.bfloat16), 'dp', scatter_dimension=0...  41.6 us
  transfers between devices with their start and end apart: 12, of which 10 were waited for; matrix products, arithmetic and copies ran while one was open for 14% of the time, Pallas kernels for 0%

commit v1 on v0

--- a/solution.py
+++ b/solution.py
@@ -46,11 +46,11 @@
         slot_count, block_part, width
     )
     select = picked.astype(jnp.bfloat16)
-    gathered = lax.all_gather(arrived, "tensor", axis=1, tiled=True)
-    neighbours = jnp.dot(
-        select, gathered.reshape(slot_count, NB * width), preferred_element_type=jnp.float32
+    live = jnp.dot(
+        select, arrived.reshape(slot_count, block_part * width), preferred_element_type=jnp.float32
     )
-    neighbours = neighbours.astype(jnp.bfloat16)
+    live = live.astype(jnp.bfloat16).reshape(live_blocks, block_part, width)
+    neighbours = lax.all_gather(live, "tensor", axis=1, tiled=True)
     nbr_flat = neighbours.reshape(live_blocks * NB, width)
     hidden_full = lax.all_gather(hidden_in, "tensor", axis=1, tiled=True)
     query = jnp.dot(hidden_full, w_query, preferred_element_type=jnp.float32).astype(jnp.bfloat16)
@@ -67,8 +67,8 @@
     attended = jnp.einsum("chqk,ckhd->cqhd", probs_b, values_h, preferred_element_type=jnp.float32)
     attended = attended.astype(jnp.bfloat16).reshape(tok_rows, columns)
     out_terms = jnp.dot(attended, w_output, preferred_element_type=jnp.float32)
-    layer_out = lax.psum_scatter(out_terms, "tensor", scatter_dimension=1, tiled=True).astype(
-        jnp.bfloat16
+    layer_out = lax.psum_scatter(
+        out_terms.astype(jnp.bfloat16), "tensor", scatter_dimension=1, tiled=True
     )
     grad_full = lax.all_gather(cotangent, "tensor", axis=1, tiled=True)
     grad_att = jnp.dot(grad_full, w_output.T, preferred_element_type=jnp.float32).astype(
@@ -88,25 +88,25 @@
     grad_k = jnp.einsum("chqk,cqhd->ckhd", grad_score, query_h, preferred_element_type=jnp.float32)
     grad_k = grad_k.astype(jnp.bfloat16).reshape(live_blocks * NB, columns)
     hidden_terms = jnp.dot(grad_q, w_query.T, preferred_element_type=jnp.float32)
-    grad_hidden = lax.psum_scatter(hidden_terms, "tensor", scatter_dimension=1, tiled=True).astype(
-        jnp.bfloat16
+    grad_hidden = lax.psum_scatter(
+        hidden_terms.astype(jnp.bfloat16), "tensor", scatter_dimension=1, tiled=True
     )
     grad_query = jnp.dot(hidden_full.T, grad_q, preferred_element_type=jnp.float32)
     grad_key = jnp.dot(nbr_flat.T, grad_k, preferred_element_type=jnp.float32)
     grad_value = jnp.dot(nbr_flat.T, grad_v, preferred_element_type=jnp.float32)
     nbr_terms = jnp.dot(grad_k, w_key.T, preferred_element_type=jnp.float32)
     nbr_terms = nbr_terms + jnp.dot(grad_v, w_value.T, preferred_element_type=jnp.float32)
-    spread_table = picked.astype(jnp.float32).T
-    spread = jnp.dot(
-        spread_table, nbr_terms.reshape(live_blocks, NB * width), precision=lax.Precision.HIGHEST
-    )
     share = lax.psum_scatter(
-        spread.reshape(slot_count, NB, width).astype(jnp.bfloat16),
+        nbr_terms.astype(jnp.bfloat16).reshape(live_blocks, NB, width),
         "tensor",
         scatter_dimension=1,
         tiled=True,
-    ).astype(jnp.float32)
-    slot_grad = share.reshape(slot_count, block_part * width)
+    )
+    slot_grad = jnp.dot(
+        select.T,
+        share.reshape(live_blocks, block_part * width),
+        preferred_element_type=jnp.float32,
+    ).astype(jnp.bfloat16)
     returned = lax.all_to_all(
         slot_grad.reshape(n_shards, capacity, block_part, width),
         "dp",
@@ -115,9 +115,9 @@
         tiled=True,
     )
     grad_encodings = jnp.dot(
-        table.astype(jnp.float32).T,
+        table.T,
         returned.reshape(slot_count, block_part * width),
-        precision=lax.Precision.HIGHEST,
+        preferred_element_type=jnp.float32,
     )
     grad_encodings = grad_encodings.reshape(db_blocks, block_part, width)
     summed_q, summed_k, summed_v, summed_o = (

time: 948 us -> 707 us (0.75)
  waiting for transfers between devices: 645 us -> 445 us
  local copies, waits for them, and re-layouts: 56.6 us -> 36.1 us
  matrix products: 178 us -> 160 us
    reduce_scatter x3, waiting for transfers between devices: 234 us -> 124 us  [the longest x1 63.1 us: shards(): lax.psum_scatter(hidden_terms.astype(jnp.bfloat16), 'tensor', scatter_dim...]
    all_gather x1, waiting for transfers between devices: 94.7 us -> 49.8 us  [shards(): neighbours = lax.all_gather(live, 'tensor', axis=1, tiled=True)]
    reduce_scatter x1, waiting for transfers between devices: 46.8 us -> 4.92 us  [shards(): lax.psum_scatter(grad_value.astype(jnp.bfloat16), 'dp', scatter_dimension...]
    dot_general x3, matrix products: 19.3 us -> 2.33 us  [the longest x1 1.23 us: shards(): jnp.dot(table.T, returned.reshape(slot_count, block_part * width), prefer...]
    reshape x2 -> x1, local copies, waits for them, and re-layouts: 10.6 us -> 0.9 us  [shards(): live = live.astype(jnp.bfloat16).reshape(live_blocks, block_part, width)]
    unnamed x33 -> x32, local copies, waits for them, and re-layouts: 29.7 us -> 22.9 us
  transfers between devices with their start and end apart: 12 -> 12, of which waited for: 10 -> 9; matrix products, arithmetic and copies ran while one was open for 14% -> 19% of each run, Pallas kernels for 0% -> 0%
where the time goes in v1:
time: 707 us; the launch traced here: 699 us
  waiting for transfers between devices  445 us (63%)
  matrix products  160 us (23%)
  local copies, waits for them, and re-layouts  36.1 us (5%)
  blocking collectives  22.8 us (3%)
  between operations  14.9 us (2%)
  other arithmetic  10.6 us (1%)
  starting transfers between devices  9.93 us (1%)
    reduce_scatter x1, waiting for transfers between devices, shards(): lax.psum_scatter(grad_output.astype(jnp.bfloat16), 'dp', scatter_dimensio...  72.2 us
    reduce_scatter x1, waiting for transfers between devices, shards(): lax.psum_scatter(grad_query.astype(jnp.bfloat16), 'dp', scatter_dimension...  64.3 us
    reduce_scatter x1, waiting for transfers between devices, shards(): lax.psum_scatter(hidden_terms.astype(jnp.bfloat16), 'tensor', scatter_dim...  63.1 us
    reduce_scatter x1, waiting for transfers between devices, shards(): lax.psum_scatter(out_terms.astype(jnp.bfloat16), 'tensor', scatter_dimens...  60.5 us
    all_gather x1, waiting for transfers between devices, shards(): hidden_full = lax.all_gather(hidden_in, 'tensor', axis=1, tiled=True)  55.7 us
    all_gather x1, waiting for transfers between devices, shards(): neighbours = lax.all_gather(live, 'tensor', axis=1, tiled=True)  49.8 us
    reduce_scatter x1, waiting for transfers between devices, shards(): lax.psum_scatter(grad_key.astype(jnp.bfloat16), 'dp', scatter_dimension=0...  47.5 us
    all_gather x1, waiting for transfers between devices, shards(): grad_full = lax.all_gather(cotangent, 'tensor', axis=1, tiled=True)  25 us
  transfers between devices with their start and end apart: 12, of which 9 were waited for; matrix products, arithmetic and copies ran while one was open for 19% of the time, Pallas kernels for 0%

profile of v1, /device:TPU:0, one launch (start us, length us, event | category | flops | bytes accessed | tf_op | source)
XLA Modules:
  0.0 699.3 jit_solution(17864073420281806789)
XLA Ops:
  11.3 5.2 all-to-all-start
  16.6 5.2 copy.83
  26.0 22.8 %all_to_all.16 = bf16[8,3,32,896]{3,2,1,0:T(8,128)(2,1)S(1)} all-to-all(bf16[8,3,32,896]{3,2,1,0:T(8,128)(2,1)S(1)} %bitcast.120), channel_id=1, replica_groups=mesh['dp'=8,'tensor'=4] {'dp'}, dimensions={0} | all-to-all | bytes 2752512 | tf_op jit(solution)/shard_map/all_to_all | solution.py:45
  50.8 25.0 %all-gather.8.cloned.1.call-done = bf16[384,4096]{1,0:T(8,128)(2,1)} async-done(((bf16[384,1024]{1,0:T(8,128)(2,1)}), bf16[384,4096]{1,0:T(8,128)(2,1)}) %all-gather.8.cloned.1.call-update) | async-done | bytes 3145744 | tf_op jit(solution)/shard_map/all_gather | solution.py:73
  75.8 7.8 %fusion.57 = bf16[48,8,8,128]{3,1,2,0:T(8,128)(2,1)S(1)} fusion(bf16[384,4096]{1,0:T(8,128)(2,1)} %all-gather.8.cloned.1.call-done, bf16[1024,4096]{1,0:T(8,128)(2,1)} %param.16), kind=kOutput, calls=%fused_computation.56 | convolution fusion | flops 3221618688 | bytes 12320768 | tf_op jit(solution)/shard_map/dot_general | solution.py:74
  83.7 55.7 %all-gather.6.cloned.1.call-done = bf16[384,4096]{1,0:T(8,128)(2,1)} async-done(((bf16[384,1024]{1,0:T(8,128)(2,1)}), bf16[384,4096]{1,0:T(8,128)(2,1)}) %all-gather.6.cloned.1.call-update) | async-done | bytes 3145744 | tf_op jit(solution)/shard_map/all_gather | solution.py:55
  139.4 7.7 %fusion.56 = bf16[48,8,8,128]{3,1,2,0:T(8,128)(2,1)S(1)} fusion(bf16[384,4096]{1,0:T(8,128)(2,1)} %all-gather.6.cloned.1.call-done, bf16[4096,1024]{1,0:T(8,128)(2,1)} %param.13), kind=kOutput, calls=%fused_computation.55 | convolution fusion | flops 3221618688 | bytes 12320768 | tf_op jit(solution)/shard_map/dot_general | solution.py:56
  147.4 49.8 %all-gather.4.cloned.1.call-done = bf16[12,128,896]{2,1,0:T(8,128)(2,1)} async-done(((bf16[12,32,896]{2,1,0:T(8,128)(2,1)}), bf16[12,128,896]{2,1,0:T(8,128)(2,1)}) %all-gather.4.cloned.1.call-update) | async-done | bytes 2752528 | tf_op jit(solution)/shard_map/all_gather | solution.py:53
  197.2 5.6 fusion.28
  205.2 3.6 fusion.27
  216.4 10.4 %convert_bitcast_fusion.1 = bf16[6,256,8,128]{1,3,2,0:T(8,128)(2,1)} fusion(bf16[6,64,8,128]{3,2,1,0:T(8,128)(2,1)S(1)} %bitcast.128, f32[6,8,64]{2,1,0:T(8,128)S(1)} %get-tuple-element.35, f32[6,8,64,256]{3,2,1,0:T(8,128)} %copy-done.3), kind=kOutput, calls=%fused_computation.19 | convolution fusion | flops 206834944 | bytes 7090176 | tf_op jit(solution)/shard_map/chqk,cqhd->ckhd/dot_general | solution.py:84
  226.9 23.5 %convert_bitcast_fusion.2 = bf16[6,256,8,128]{1,3,2,0:T(8,128)(2,1)} fusion(f32[6,8,64,256]{3,2,1,0:T(8,128)} %fusion.14, bf16[6,64,8,128]{3,2,1,0:T(8,128)(2,1)S(1)} %bitcast.130, f32[6,8,64,256]{3,2,1,0:T(8,128)} %get-tuple-element.36, f32[6,8,64]{2,1,0:T(8,128)S(1)} %get-tuple-element.35), kind=kOutput, calls=%fused_computation.20 | convolution fusion | flops 208407808 | bytes 10235904 | tf_op jit(solution)/shard_map/chqk,cqhd->ckhd/dot_general | solution.py:88
  250.3 4.9 copy.75
  255.2 4.8 copy.77
  260.0 5.5 fusion.7
  265.6 4.8 add_convert_fusion
  270.5 7.0 %fusion.36 = bf16[896,1024]{1,0:T(8,128)(2,1)} fusion(bf16[1536,896]{1,0:T(8,128)(2,1)} %bitcast.142, bf16[192,8,8,128]{3,2,1,0:T(8,128)(2,1)} %bitcast.133), kind=kOutput, calls=%fused_computation.42 | convolution fusion | flops 2819489792 | bytes 7733248 | tf_op jit(solution)/shard_map/dot_general | solution.py:96
  277.7 7.0 %fusion.33 = bf16[896,1024]{1,0:T(8,128)(2,1)} fusion(bf16[1536,896]{1,0:T(8,128)(2,1)} %bitcast.143, bf16[192,8,8,128]{3,2,1,0:T(8,128)(2,1)} %bitcast.132), kind=kOutput, calls=%fused_computation.41 | convolution fusion | flops 2819489792 | bytes 7733248 | tf_op jit(solution)/shard_map/dot_general | solution.py:95
  284.8 22.6 %fusion.58 = bf16[6,64,8,128]{3,1,2,0:T(8,128)(2,1)S(1)} fusion(bf16[6,256,8,128]{3,2,1,0:T(8,128)(2,1)} %bitcast.116, f32[6,8,64,256]{3,2,1,0:T(8,128)} %fusion.14, f32[6,8,64,256]{3,2,1,0:T(8,128)} %get-tuple-element.36, f32[6,8,64]{2,1,0:T(8,128)S(1)} %get-tuple-element.35), kind=kOutput, calls=%fused_computation.57 | convolution fusion | flops 207228160 | bytes 10235904 | tf_op jit(solution)/shard_map/chqk,ckhd->cqhd/dot_general | solution.py:86
  308.0 8.7 %convert_bitcast_fusion = bf16[4096,1024]{0,1:T(8,128)(2,1)} fusion(bf16[384,4096]{1,0:T(8,128)(2,1)} %all-gather.6.cloned.1.call-done, bf16[48,8,8,128]{3,2,1,0:T(8,128)(2,1)S(1)} %bitcast.137), kind=kOutput, calls=%fused_computation.5 | convolution fusion | flops 3225419776 | bytes 12320768 | tf_op jit(solution)/shard_map/dot_general | solution.py:94
  316.9 9.3 %fusion.53 = bf16[6,64,8,128]{3,1,2,0:T(8,128)(2,1)S(1)} fusion(bf16[6,256,8,128]{3,2,1,0:T(8,128)(2,1)} %bitcast.114, f32[6,8,64]{2,1,0:T(8,128)S(1)} %get-tuple-element.35, f32[6,8,64,256]{3,2,1,0:T(8,128)} %copy-done.3), kind=kOutput, calls=%fused_computation.54 | convolution fusion | flops 205655296 | bytes 7090176 | tf_op jit(solution)/shard_map/chqk,ckhd->cqhd/dot_general | solution.py:67
  326.7 8.8 %convolution_convert_fusion.3 = bf16[1024,4096]{1,0:T(8,128)(2,1)} fusion(bf16[384,4096]{1,0:T(8,128)(2,1)} %all-gather.8.cloned.1.call-done, bf16[48,8,8,128]{3,2,1,0:T(8,128)(2,1)S(1)} %bitcast.139), kind=kOutput, calls=%fused_computation.6 | convolution fusion | flops 3225419776 | bytes 12320768 | tf_op jit(solution)/shard_map/dot_general | solution.py:77
  335.6 8.5 %convolution_convert_fusion.5 = bf16[384,4096]{1,0:T(8,128)(2,1)} fusion(bf16[1024,4096]{1,0:T(8,128)(2,1)} %param.16, bf16[48,8,8,128]{3,2,1,0:T(8,128)(2,1)S(1)} %bitcast.140), kind=kOutput, calls=%fused_computation.8 | convolution fusion | flops 3222798336 | bytes 12320768 | tf_op jit(solution)/shard_map/dot_general | solution.py:69
  344.2 10.4 %convolution_convert_fusion.4 = bf16[384,4096]{1,0:T(8,128)(2,1)} fusion(bf16[4096,1024]{1,0:T(8,128)(2,1)} %param.13, bf16[48,8,8,128]{3,2,1,0:T(8,128)(2,1)S(1)} %bitcast.138), kind=kOutput, calls=%fused_computation.7 | convolution fusion | flops 3222798336 | bytes 12320768 | tf_op jit(solution)/shard_map/dot_general | solution.py:90
  358.0 3.9 all-to-all-start.2
  362.0 4.9 reduce-scatter.18.cloned.1.call-done
  368.7 47.5 %reduce-scatter.16.cloned.1.call-done = bf16[112,1024]{1,0:T(8,128)(2,1)} async-done(((bf16[896,1024]{1,0:T(8,128)(2,1)}), bf16[112,1024]{1,0:T(8,128)(2,1)}) %reduce-scatter.16.cloned.1.call-update) | async-done | bytes 229392 | tf_op jit(solution)/shard_map/reduce_scatter | solution.py:127
  419.1 7.5 %copy.79 = f32[64,32,896]{2,1,0:T(8,128)} copy(f32[64,32,896]{2,0,1:T(8,128)S(1)} %fusion.50) | data formatting | bytes 14680064
  426.6 64.3 %reduce-scatter.14.cloned.1.call-done = bf16[512,1024]{0,1:T(8,128)(2,1)} async-done(((bf16[4096,1024]{0,1:T(8,128)(2,1)}), bf16[512,1024]{0,1:T(8,128)(2,1)}) %reduce-scatter.14.cloned.1.call-update) | async-done | bytes 1048592 | tf_op jit(solution)/shard_map/reduce_scatter | solution.py:124
  493.5 72.2 %reduce-scatter.20.cloned.1.call-done = bf16[1024,512]{1,0:T(8,128)(2,1)} async-done(((bf16[1024,4096]{1,0:T(8,128)(2,1)}), bf16[1024,512]{1,0:T(8,128)(2,1)}) %reduce-scatter.20.cloned.1.call-update) | async-done | bytes 1048592 | tf_op jit(solution)/shard_map/reduce_scatter | solution.py:133
  568.5 60.5 %reduce-scatter.8.cloned.1.call-done = bf16[384,1024]{1,0:T(8,128)(2,1)} async-done(((bf16[384,4096]{1,0:T(8,128)(2,1)}), bf16[384,1024]{1,0:T(8,128)(2,1)}) %reduce-scatter.8.cloned.1.call-update) | async-done | bytes 786448 | tf_op jit(solution)/shard_map/reduce_scatter | solution.py:70
  629.0 63.1 %reduce-scatter.10.cloned.1.call-done = bf16[384,1024]{1,0:T(8,128)(2,1)} async-done(((bf16[384,4096]{1,0:T(8,128)(2,1)}), bf16[384,1024]{1,0:T(8,128)(2,1)}) %reduce-scatter.10.cloned.1.call-update) | async-done | bytes 786448 | tf_op jit(solution)/shard_map/reduce_scatter | solution.py:91
  (78 shorter events, 35.8 us)
Async XLA Ops:
  7.2 190.0 %copy-start = (bf16[896,1024]{1,0:T(8,128)(2,1)S(1)}, bf16[896,1024]{1,0:T(8,128)(2,1)}, u32[]{:S(2)}) copy-start(bf16[896,1024]{1,0:T(8,128)(2,1)} %param.14) | copy-start | bytes 5505028
  7.2 68.6 %all-gather.8.cloned.1.call-start = ((), (), s32[]{:S(2)}) async-start(), calls=%async_computation.13 | async-start | bytes 3932160 | tf_op jit(solution)/shard_map/all_gather | solution.py:73
  7.9 131.5 %all-gather.6.cloned.1.call-start = ((), (), s32[]{:S(2)}) async-start(), calls=%async_computation.11 | async-start | bytes 3932160 | tf_op jit(solution)/shard_map/all_gather | solution.py:55
  11.3 10.5 %all-to-all-start = ((s32[8,1,3]{2,1,0:T(1,128)}), s32[8,1,3]{2,1,0:T(1,128)S(1)}, u32[]{:S(2)}, u32[]{:S(2)}) async-start(s32[8,1,3]{2,1,0:T(1,128)} %bitcast), calls=%async_computation | async-start | bytes 8192 | tf_op jit(solution)/shard_map/all_to_all | solution.py:35
  16.5 180.7 %all-gather.4.cloned.1.call-start = ((), (), s32[]{:S(2)}) async-start(), calls=%async_computation.10 | async-start | bytes 3440640 | tf_op jit(solution)/shard_map/all_gather | solution.py:53
  50.7 303.9 %reduce-scatter.12.cloned.1.call-start = ((), (), s32[]{:S(2)}) async-start(), calls=%async_computation.15 | async-start | bytes 3440640 | tf_op jit(solution)/shard_map/reduce_scatter | solution.py:99
  202.8 1.8 copy-start.6
  202.8 2.3 copy-start.7
  205.2 4.4 copy-start.4
  209.6 3.9 copy-start.2
  210.8 2.7 copy-start.3
  260.0 5.5 copy-start.5
  260.0 5.5 copy-start.8
  270.4 96.5 %reduce-scatter.18.cloned.1.call-start = ((), (), s32[]{:S(2)}) async-start(), calls=%async_computation.18 | async-start | bytes 2064384 | tf_op jit(solution)/shard_map/reduce_scatter | solution.py:130
  277.5 138.6 %reduce-scatter.16.cloned.1.call-start = ((), (), s32[]{:S(2)}) async-start(), calls=%async_computation.17 | async-start | bytes 2064384 | tf_op jit(solution)/shard_map/reduce_scatter | solution.py:127
  284.8 206.1 %reduce-scatter.14.cloned.1.call-start = ((), (), s32[]{:S(2)}) async-start(), calls=%async_computation.16 | async-start | bytes 9437184 | tf_op jit(solution)/shard_map/reduce_scatter | solution.py:124
  316.7 249.0 %reduce-scatter.20.cloned.1.call-start = ((), (), s32[]{:S(2)}) async-start(), calls=%async_computation.19 | async-start | bytes 9437184 | tf_op jit(solution)/shard_map/reduce_scatter | solution.py:133
  335.6 293.4 %reduce-scatter.8.cloned.1.call-start = ((), (), s32[]{:S(2)}) async-start(), calls=%async_computation.12 | async-start | bytes 3932160 | tf_op jit(solution)/shard_map/reduce_scatter | solution.py:70
  344.2 347.9 %reduce-scatter.10.cloned.1.call-start = ((), (), s32[]{:S(2)}) async-start(), calls=%async_computation.14 | async-start | bytes 3932160 | tf_op jit(solution)/shard_map/reduce_scatter | solution.py:91
  358.0 59.8 %all-to-all-start.2 = ((bf16[8,3,32,896]{3,2,1,0:T(8,128)(2,1)}), bf16[8,3,32,896]{3,2,1,0:T(8,128)(2,1)S(1)}, u32[]{:S(2)}, u32[]{:S(2)}) async-start(bf16[8,3,32,896]{3,2,1,0:T(8,128)(2,1)} %bitcast.52), calls=%async_computation.5 | async-start | bytes 2752512 | tf_op jit(solution)/shard_map/all_to_all | solution.py:110
  419.1 273.0 %copy-start.1 = (bf16[896,1024]{1,0:T(8,128)(2,1)S(1)}, bf16[896,1024]{1,0:T(8,128)(2,1)}, u32[]{:S(2)}) copy-start(bf16[896,1024]{1,0:T(8,128)(2,1)} %param.14) | copy-start | bytes 5505028
Sparse Core Ops, SparseCore 0:
  9.6 66.1 all-gather.7
  77.3 62.0 all-gather.5
  141.6 55.5 all-gather.3
  270.6 53.0 reduce-scatter.11
  327.4 39.4 reduce-scatter.17
  370.7 45.3 reduce-scatter.15
  419.6 71.2 reduce-scatter.13
  494.3 71.2 reduce-scatter.19
  568.6 60.3 reduce-scatter.7
  631.7 60.2 reduce-scatter.9
